TPU v7x, 256 devices: a whole 4x4x8 slice. The times are simulated.
256 devices in a mesh: head: 4 (over x), blk: 64 (over y, z, core).
Axes of the slice: x: 4, y: 4, z: 8, core: 2. Of those that a mesh axis runs over, the one named last changes fastest.
Arguments:
- doc_x: bfloat16 [65536, 1024], P('blk'), may hold values from -6 to 6
- doc_seg: int32 [65536], P('blk'), may hold values from 0 to 1023, as said below
- doc_query: int32 [1024], replicated, may hold values from 0 to 7
- doc_var: int32 [65536], P('blk'), may hold values from 0 to 7
- query_len: int32 [8], replicated, may hold values from 256 to 4096, as said below
- block_perm: int32 [64], replicated, may hold values from 0 to 63, each once
- cache_k: bfloat16 [32768, 1024], P('blk', 'head'), may hold values from -164 to 164
- cache_v: bfloat16 [32768, 1024], P('blk', 'head'), may hold values from -6 to 6
- cache_var: int32 [32768], P('blk'), may hold values from 0 to 7
- w_query: bfloat16 [1024, 1024], P(None, 'head'), may hold values from -0.1875 to 0.1875
- w_key: bfloat16 [1024, 1024], P(None, 'head'), may hold values from -0.5 to 0.5
- w_value: bfloat16 [1024, 1024], P(None, 'head'), may hold values from -0.1875 to 0.1875
- w_out: bfloat16 [1024, 1024], P('head'), may hold values from -0.1875 to 0.1875
- var_bias: float32 [2, 16], P(None, 'head'), may hold values from -1 to 1
- norm_gain: float32 [1024], replicated, may hold values from 0.1 to 1.9
- readout: float32 [1024], replicated, may hold values from -1.5 to 1.5
Outputs:
- update: float32 [65536, 1024], P('blk', 'head')
- pooled: float32 [1024], P('blk')
Inputs may be any that keep to these rules, and one draw needn't show every extreme that they name: `doc_seg`: index i of blk holds documents i * 16 to (i + 1) * 16 - 1 whole; its 1024 tokens form 8 runs of 128 tokens, run j holding its documents 2j and 2j + 1, both of one query, and the 8 runs of one index belong to 8 different queries. query_len[0] = 4096.
All inputs are finite; a program needn't handle non-finite values.
Results may differ from a plain program's by a relative error of at most 0.012.
The roundings to bfloat16 on the way count: a program that leaves them out, or rounds other values in their place, can miss the bound.
Values may be sent and summed in bfloat16 or wider, within the bound.
A program may use at most 128 MiB of HBM per device.

v0:
```python
import jax
import jax.numpy as jnp
from jax import lax
from jax.sharding import PartitionSpec as P

D = 1024
DH = 64
QUERIES = 8


def rotary(projected, positions):
    row_count = projected.shape[0]
    head_count = projected.shape[1] // DH
    half_size = DH // 2
    shaped = projected.reshape(row_count, head_count, DH)
    frequency = 10000.0 ** (-jnp.arange(half_size, dtype=jnp.float32) / half_size)
    angles = positions.astype(jnp.float32)[:, None] * frequency[None, :]
    cosine = jnp.cos(angles)[:, None, :]
    sine_part = jnp.sin(angles)[:, None, :]
    first_half = shaped[:, :, :half_size]
    second_half = shaped[:, :, half_size:]
    turned = jnp.concatenate(
        [
            first_half * cosine - second_half * sine_part,
            second_half * cosine + first_half * sine_part,
        ],
        axis=2,
    )
    return turned.reshape(row_count, head_count * DH)


def softmax_part(scores, allowed):
    scores = jnp.where(allowed, scores, -1e30)
    peak = jnp.max(scores, axis=-1)
    weights = jnp.where(allowed, jnp.exp(scores - peak[..., None]), 0.0)
    return (peak, jnp.sum(weights, axis=-1), weights.astype(jnp.bfloat16))


def cache_part(
    recv_q, recv_var, cache_keys, cache_values, cache_var, row_valid, bias_same, bias_other
):
    source_count = recv_q.shape[0]
    item_count = recv_q.shape[1]
    col_count = recv_q.shape[2]
    head_count = cache_keys.shape[1]
    total_rows = source_count * item_count
    block_rows = 512
    block_count = total_rows // block_rows
    flat_q = recv_q.reshape(block_count, block_rows, head_count, DH)
    flat_var = recv_var.reshape(block_count, block_rows).astype(jnp.int32)

    def one_block(block_inputs):
        block_q, block_var = block_inputs
        scores = (
            jnp.einsum("thd,rhd->htr", block_q, cache_keys, preferred_element_type=jnp.float32)
            * 0.125
        )
        scores = scores + jnp.where(
            (block_var[:, None] == cache_var[None, :])[None], bias_same, bias_other
        )
        allowed = jnp.broadcast_to(row_valid[None, None, :], scores.shape)
        peak, total_weight, weights = softmax_part(scores, allowed)
        mixed = jnp.einsum(
            "htr,rhd->thd", weights, cache_values, preferred_element_type=jnp.float32
        )
        return (peak.T, total_weight.T, mixed.reshape(block_rows, col_count))

    maxima, totals, sums = lax.map(one_block, (flat_q, flat_var))
    return (
        maxima.reshape(source_count, item_count, head_count),
        totals.reshape(source_count, item_count, head_count),
        sums.reshape(source_count, item_count, col_count),
    )


def body(
    doc_x,
    doc_seg,
    doc_query,
    doc_var,
    query_len,
    block_perm,
    cache_k,
    cache_v,
    cache_var,
    w_query,
    w_key,
    w_value,
    w_out,
    var_bias,
    norm_gain,
    readout,
):
    row_count = doc_x.shape[0]
    col_count = w_query.shape[1]
    head_count = col_count // DH
    cache_count = cache_k.shape[0]
    blk_count = lax.axis_size("blk")
    blk_index = lax.axis_index("blk")
    head_index = lax.axis_index("head")
    blocks_each = blk_count // QUERIES
    slot_count = QUERIES
    slot_rows = row_count // slot_count
    doc_count = 2 * slot_count
    first_doc = blk_index * doc_count
    local_seg = doc_seg - first_doc
    member = (local_seg[:, None] == jnp.arange(doc_count, dtype=jnp.int32)[None, :]).astype(
        jnp.int32
    )
    lengths = jnp.sum(member, axis=0)
    starts = jnp.cumsum(lengths) - lengths
    first_pos = jnp.dot(member, starts)
    own_docs_query = lax.dynamic_slice_in_dim(doc_query, first_doc, doc_count)
    query_table = (own_docs_query[:, None] == jnp.arange(QUERIES, dtype=jnp.int32)[None, :]).astype(
        jnp.int32
    )
    doc_len = jnp.sum(query_table * query_len[None, :], axis=1)
    tok_len = jnp.dot(member, doc_len)
    positions = tok_len + jnp.arange(row_count, dtype=jnp.int32) - first_pos
    query_rot = rotary(
        jnp.dot(doc_x, w_query, preferred_element_type=jnp.float32), positions
    ).astype(jnp.bfloat16)
    key_rot = rotary(jnp.dot(doc_x, w_key, preferred_element_type=jnp.float32), positions).astype(
        jnp.bfloat16
    )
    value_proj = jnp.dot(doc_x, w_value, preferred_element_type=jnp.float32).astype(jnp.bfloat16)
    bias_same = var_bias[0][:, None, None]
    bias_other = var_bias[1][:, None, None]
    shaped_q = query_rot.reshape(slot_count, slot_rows, head_count, DH)
    shaped_k = key_rot.reshape(slot_count, slot_rows, head_count, DH)
    shaped_v = value_proj.reshape(slot_count, slot_rows, head_count, DH)
    slot_seg = local_seg.reshape(slot_count, slot_rows)
    slot_var = doc_var.reshape(slot_count, slot_rows)
    self_scores = (
        jnp.einsum("gthd,gshd->ghts", shaped_q, shaped_k, preferred_element_type=jnp.float32)
        * 0.125
    )
    self_scores = self_scores + jnp.where(
        (slot_var[:, :, None] == slot_var[:, None, :])[:, None], bias_same[None], bias_other[None]
    )
    self_allowed = (slot_seg[:, :, None] == slot_seg[:, None, :])[:, None]
    self_peak, self_total, self_weights = softmax_part(self_scores, self_allowed)
    self_sum = jnp.einsum(
        "ghts,gshd->gthd", self_weights, shaped_v, preferred_element_type=jnp.float32
    )
    self_peak = self_peak.transpose(0, 2, 1)
    self_total = self_total.transpose(0, 2, 1)
    slot_query = own_docs_query.reshape(slot_count, 2)[:, 0]
    block_query = block_perm // blocks_each
    slot_match = block_query[:, None] == slot_query[None, :]
    slot_pick = jnp.sum(
        slot_match.astype(jnp.int32) * jnp.arange(slot_count, dtype=jnp.int32)[None, :], axis=1
    )
    send_q = jnp.take(query_rot.reshape(slot_count, slot_rows, col_count), slot_pick, axis=0)
    send_var = jnp.take(slot_var, slot_pick, axis=0).astype(jnp.bfloat16)
    my_block = lax.dynamic_slice_in_dim(block_perm, blk_index, 1)[0]
    my_query = my_block // blocks_each
    first_row = my_block % blocks_each * cache_count
    my_len = lax.dynamic_slice_in_dim(query_len, my_query, 1)[0]
    row_valid = first_row + jnp.arange(cache_count, dtype=jnp.int32) < my_len
    cache_keys = cache_k.reshape(cache_count, head_count, DH)
    cache_values = cache_v.reshape(cache_count, head_count, DH)
    recv_q, recv_var = (
        lax.all_to_all(send_q, "blk", split_axis=0, concat_axis=0, tiled=True),
        lax.all_to_all(send_var, "blk", split_axis=0, concat_axis=0, tiled=True),
    )
    maxima, totals, sums = cache_part(
        recv_q, recv_var, cache_keys, cache_values, cache_var, row_valid, bias_same, bias_other
    )
    got_max, got_total, got_sum = (
        lax.all_to_all(maxima, "blk", split_axis=0, concat_axis=0, tiled=True),
        lax.all_to_all(totals, "blk", split_axis=0, concat_axis=0, tiled=True),
        lax.all_to_all(sums, "blk", split_axis=0, concat_axis=0, tiled=True),
    )
    match_float = slot_match.astype(jnp.float32)
    spread_max = jnp.where(slot_match[:, :, None, None], got_max[:, None], -1e30)
    cache_peak = jnp.max(spread_max, axis=0)
    peak = jnp.maximum(cache_peak, self_peak)
    device_peak = jnp.take(peak, slot_pick, axis=0)
    factor = jnp.exp(got_max - device_peak)
    cache_total = jnp.einsum(
        "dg,dth->gth", match_float, got_total * factor, precision=lax.Precision.HIGHEST
    )
    scaled_sum = got_sum.reshape(blk_count, slot_rows, head_count, DH) * factor[..., None]
    cache_sum = jnp.einsum(
        "dg,dthe->gthe", match_float, scaled_sum, precision=lax.Precision.HIGHEST
    )
    self_factor = jnp.exp(self_peak - peak)
    numerator = cache_sum + self_sum * self_factor[..., None]
    denominator = cache_total + self_total * self_factor
    attended = (
        (numerator / denominator[..., None]).reshape(row_count, col_count).astype(jnp.bfloat16)
    )
    partial_update = jnp.dot(attended, w_out, preferred_element_type=jnp.float32)
    x_float = doc_x.astype(jnp.float32)
    whole_sum = lax.psum(partial_update, "head")
    hidden = x_float + whole_sum
    square_sum = jnp.sum(hidden * hidden, axis=1)
    weighted = jnp.sum(hidden * norm_gain * readout, axis=1)
    update = lax.dynamic_slice_in_dim(whole_sum, head_index * col_count, col_count, 1)
    token_score = weighted * lax.rsqrt(square_sum / D + 1e-06)
    pooled_sum = jnp.dot(token_score, member.astype(jnp.float32), precision=lax.Precision.HIGHEST)
    return (update, pooled_sum / lengths.astype(jnp.float32))


def solution(mesh):
    return jax.shard_map(
        body,
        mesh=mesh,
        in_specs=(
            P("blk", None),
            P("blk"),
            P(),
            P("blk"),
            P(),
            P(),
            P("blk", "head"),
            P("blk", "head"),
            P("blk"),
            P(None, "head"),
            P(None, "head"),
            P(None, "head"),
            P("head", None),
            P(None, "head"),
            P(),
            P(),
        ),
        out_specs=(P("blk", "head"), P("blk")),
        check_vma=False,
    )
```

profile of v0, /device:TPU:1, one launch (start us, length us, event | category | flops | bytes accessed | tf_op | source)
XLA Modules:
  0.0 646.7 jit_solution(2000789111802115484)
XLA Ops:
  11.0 13.2 %all-to-all-start.1 = ((bf16[64,1,128]{2,1,0:T(2,128)(2,1)}), bf16[64,1,128]{2,1,0:T(2,128)(2,1)S(1)}, u32[]{:S(2)}, u32[]{:S(2)}) async-start(bf16[64,1,128]{2,1,0:T(2,128)(2,1)} %copy.100), calls=%async_computation.1 | async-start | bytes 65536 | tf_op jit(solution)/shard_map/all_to_all | solution.py:165
  26.4 2.4 fusion.63
  30.1 2.8 gather_fusion
  32.8 4.6 broadcast_select_fusion
  37.4 10.7 %all-to-all-start = ((bf16[64,128,256]{2,1,0:T(8,128)(2,1)}), bf16[64,128,256]{2,1,0:T(8,128)(2,1)}, u32[]{:S(2)}, u32[]{:S(2)}) async-start(bf16[64,128,256]{2,1,0:T(8,128)(2,1)} %broadcast_select_fusion), calls=%async_computation | async-start | bytes 8388608 | tf_op jit(solution)/shard_map/all_to_all | solution.py:164
  53.1 90.9 %all-to-all-done = bf16[64,128,256]{2,1,0:T(8,128)(2,1)} async-done(((bf16[64,128,256]{2,1,0:T(8,128)(2,1)}), bf16[64,128,256]{2,1,0:T(8,128)(2,1)}, u32[]{:S(2)}, u32[]{:S(2)}) %all-to-all-start) | async-done | bytes 4194336 | tf_op jit(solution)/shard_map/all_to_all | solution.py:164
  144.0 12.9 %reshape.307 = bf16[16,512,4,64]{3,2,1,0:T(4,128)(2,1)} reshape(bf16[64,128,256]{2,1,0:T(8,128)(2,1)} %all-to-all-done) | data formatting | bytes 8388608 | tf_op jit(solution)/shard_map/reshape | solution.py:49
  156.9 12.7 %copy.102 = bf16[16,512,4,64]{1,3,2,0:T(8,128)(2,1)} copy(bf16[16,512,4,64]{3,2,1,0:T(4,128)(2,1)} %reshape.307) | data formatting | bytes 8388608
  169.6 122.0 %while.15 = (s32[]{:T(128)}, f32[16,512,4]{1,2,0:T(4,128)S(1)}, f32[16,512,4]{1,2,0:T(4,128)S(1)}, f32[16,512,256]{2,1,0:T(8,128)}, bf16[16,512,4,64]{1,3,2,0:T(...) while((s32[]{:T(128)}, f32[16,512,4]{1,2,0:T(4,128)S(1)}, ...), condition=%wide.region_7.8_spmd.clone, body=%wide.region_4.7_spmd.clone.sunk | while | flops 288617472 | bytes 17115396 | solution.py:68
  170.6 2.5 fusion.87
  174.5 1.7 fusion.89
  178.2 2.4 fusion.87
  182.1 1.7 fusion.89
  185.9 2.4 fusion.87
  193.5 2.5 fusion.87
  197.4 1.7 fusion.89
  201.1 2.5 fusion.87
  208.7 2.5 fusion.87
  212.6 1.7 fusion.89
  216.3 2.5 fusion.87
  220.3 1.7 fusion.89
  223.9 2.5 fusion.87
  231.5 2.5 fusion.87
  235.5 1.7 fusion.89
  239.2 2.4 fusion.87
  243.1 1.7 fusion.89
  246.8 2.5 fusion.87
  254.4 2.5 fusion.87
  262.0 2.5 fusion.87
  266.0 1.7 fusion.89
  269.6 2.5 fusion.87
  277.3 2.5 fusion.87
  281.2 1.7 fusion.89
  284.9 2.5 fusion.87
  291.6 16.0 %all_to_all.26 = f32[64,128,4]{1,2,0:T(4,128)} all-to-all(f32[64,128,4]{1,2,0:T(4,128)S(1)} %bitcast.155), channel_id=1, replica_groups=mesh['head'=4,'blk'=64] {'blk'}, dimensions={0} | all-to-all | bytes 262144 | tf_op jit(solution)/shard_map/all_to_all | solution.py:172
  307.6 15.0 %all_to_all.27 = f32[64,128,4]{1,2,0:T(4,128)S(1)} all-to-all(f32[64,128,4]{1,2,0:T(4,128)S(1)} %bitcast.154), channel_id=1, replica_groups=mesh['head'=4,'blk'=64] {'blk'}, dimensions={0} | all-to-all | bytes 262144 | tf_op jit(solution)/shard_map/all_to_all | solution.py:171
  322.6 5.6 all-to-all-start.2
  330.0 2.5 convolution_convert_fusion
  332.5 2.8 reshape.308
  335.7 1.8 fusion.64
  342.1 172.0 %all-to-all-done.2 = f32[64,128,256]{2,1,0:T(8,128)} async-done(((f32[64,128,256]{2,1,0:T(8,128)}), f32[64,128,256]{2,1,0:T(8,128)}, u32[]{:S(2)}, u32[]{:S(2)}) %all-to-all-start.2) | async-done | bytes 8388640 | tf_op jit(solution)/shard_map/all_to_all | solution.py:173
  514.1 9.0 %copy.104 = f32[64,128,256]{1,2,0:T(8,128)} copy(f32[64,128,256]{2,1,0:T(8,128)} %all-to-all-done.2) | data formatting | bytes 16777216 | tf_op jit(solution)/shard_map/all_to_all | solution.py:173
  523.0 4.6 broadcast_multiply_fusion
  527.7 8.5 %fusion.24 = bf16[8,128,4,64]{1,0,3,2:T(8,128)(2,1)S(1)} fusion(f32[64,128,4,64]{1,3,2,0:T(8,128)S(1)} %broadcast_multiply_fusion, f32[8,4,64,128]{3,2,1,0:T(8,128)S(1)} %copy-done.3, f32[8,128,4]{1,0,2:T(8,128)S(1)} %convolution_add_fusion, f32[8,128,4]{1,0,2:T(8,128)S(1)} %get-tuple-element.189, s32[64]{0:T(128)S(1)} %copy-done.16, s32[8]{0:T(128)S(1)} %copy-done.13), kind=kOutput, calls=%fused_computation.36 | convolution fusion | flops 202375680 | bytes 9994528 | tf_op jit(solution)/shard_map/dg,dthe->gthe/dot_general | solution.py:185
  536.2 2.7 fusion.34
  539.0 94.6 %all-reduce.2.cloned.1.call-done = f32[1024,1024]{1,0:T(8,128)} async-done(((f32[1024,1024]{1,0:T(8,128)}), f32[1024,1024]{1,0:T(8,128)}) %all-reduce.2.cloned.1.call-update) | async-done | bytes 4194320 | tf_op jit(solution)/shard_map/psum | solution.py:196
  633.6 3.3 multiply_reduce_fusion
  637.6 2.3 constant_dynamic-slice_fusion.1
  (231 shorter events, 83.7 us)
Async XLA Ops:
  7.2 529.0 %copy-start = (bf16[256,1024]{1,0:T(8,128)(2,1)S(1)}, bf16[256,1024]{1,0:T(8,128)(2,1)}, u32[]{:S(2)}) copy-start(bf16[256,1024]{1,0:T(8,128)(2,1)} %param.30) | copy-start | bytes 1572868
  7.9 320.7 %copy-start.15 = (s32[64]{0:T(128)}, s32[64]{0:T(128)S(1)}, u32[]{:S(2)}) copy-start(s32[64]{0:T(128)S(1)} %and_select_fusion) | copy-start | bytes 772
  8.9 319.7 %copy-start.12 = (s32[8]{0:T(128)}, s32[8]{0:T(128)S(1)}, u32[]{:S(2)}) copy-start(s32[8]{0:T(128)S(1)} %slice_reduce_fusion) | copy-start | bytes 100
  9.0 23.9 %copy-start.17 = (pred[64]{0:T(512)(128)(4,1)}, pred[64]{0:T(512)(128)(4,1)S(1)}, u32[]{:S(2)}) copy-start(pred[64]{0:T(512)(128)(4,1)S(1)} %compare_and_fusion) | copy-start | bytes 196
  9.0 21.1 %copy-start.14 = (s32[1024]{0:T(1024)}, s32[1024]{0:T(1024)S(1)}, u32[]{:S(2)}) copy-start(s32[1024]{0:T(1024)S(1)} %pad_clamp_fusion) | copy-start | bytes 12292
  11.0 26.4 %all-to-all-start.1 = ((bf16[64,1,128]{2,1,0:T(2,128)(2,1)}), bf16[64,1,128]{2,1,0:T(2,128)(2,1)S(1)}, u32[]{:S(2)}, u32[]{:S(2)}) async-start(bf16[64,1,128]{2,1,0:T(2,128)(2,1)} %copy.100), calls=%async_computation.1 | async-start | bytes 65536 | tf_op jit(solution)/shard_map/all_to_all | solution.py:165
  24.9 4.8 copy-start.10
  25.0 0.5 copy-start.21
  37.4 10.7 %copy-start.26 = (s32[64]{0:T(128)S(1)}, s32[64]{0:T(128)}, u32[]{:S(2)}) copy-start(s32[64]{0:T(128)} %param.23) | copy-start | bytes 772
  37.4 13.9 %copy-start.6 = (bf16[512,256]{1,0:T(8,128)(2,1)S(1)}, bf16[512,256]{1,0:T(8,128)(2,1)}, u32[]{:S(2)}) copy-start(bf16[512,256]{1,0:T(8,128)(2,1)} %param.24) | copy-start | bytes 786436
  37.4 14.1 %copy-start.7 = (bf16[512,256]{1,0:T(8,128)(2,1)S(1)}, bf16[512,256]{1,0:T(8,128)(2,1)}, u32[]{:S(2)}) copy-start(bf16[512,256]{1,0:T(8,128)(2,1)} %param.25) | copy-start | bytes 786436
  37.4 14.3 %copy-start.27 = (s32[8]{0:T(128)S(1)}, s32[8]{0:T(128)}, u32[]{:S(2)}) copy-start(s32[8]{0:T(128)} %param.22) | copy-start | bytes 100
  37.4 14.9 %copy-start.23 = (f32[2,4]{1,0:T(2,128)S(1)}, f32[2,4]{1,0:T(2,128)}, u32[]{:S(2)}) copy-start(f32[2,4]{1,0:T(2,128)} %param.31) | copy-start | bytes 100
  37.4 106.5 %all-to-all-start = ((bf16[64,128,256]{2,1,0:T(8,128)(2,1)}), bf16[64,128,256]{2,1,0:T(8,128)(2,1)}, u32[]{:S(2)}, u32[]{:S(2)}) async-start(bf16[64,128,256]{2,1,0:T(8,128)(2,1)} %broadcast_select_fusion), calls=%async_computation | async-start | bytes 8388608 | tf_op jit(solution)/shard_map/all_to_all | solution.py:164
  156.9 12.7 %copy-start.8 = (s32[512]{0:T(512)S(1)}, s32[512]{0:T(512)}, u32[]{:S(2)}) copy-start(s32[512]{0:T(512)} %param.26) | copy-start | bytes 6148
  322.6 7.4 %copy-start.1 = (bf16[1024,1024]{1,0:T(8,128)(2,1)S(1)}, bf16[1024,1024]{1,0:T(8,128)(2,1)}, u32[]{:S(2)}) copy-start(bf16[1024,1024]{1,0:T(8,128)(2,1)} %param.18) | copy-start | bytes 6291460
  322.6 191.5 %all-to-all-start.2 = ((f32[64,128,256]{2,1,0:T(8,128)}), f32[64,128,256]{2,1,0:T(8,128)}, u32[]{:S(2)}, u32[]{:S(2)}) async-start(f32[64,128,256]{2,1,0:T(8,128)} %bitcast.145), calls=%async_computation.2 | async-start | bytes 16777216 | tf_op jit(solution)/shard_map/all_to_all | solution.py:173
  328.3 7.0 %copy-start.9 = (s32[1024]{0:T(1024)S(1)}, s32[1024]{0:T(1024)}, u32[]{:S(2)}) copy-start(s32[1024]{0:T(1024)} %param.19) | copy-start | bytes 12292
  328.3 7.0 %copy-start.2 = (s32[1024]{0:T(1024)S(1)}, s32[1024]{0:T(1024)}, u32[]{:S(2)}) copy-start(s32[1024]{0:T(1024)} %param.21) | copy-start | bytes 12292
  328.3 305.3 %all-reduce.2.cloned.1.call-start = ((), (), s32[]{:S(2)}) async-start(), calls=%async_computation.5 | async-start | bytes 8388608 | tf_op jit(solution)/shard_map/psum | solution.py:196
  335.3 2.4 copy-start.24
  335.3 2.4 copy-start.25
  337.7 1.3 copy-start.4
  340.8 1.0 copy-start.5
  340.8 1.0 copy-start.18
  340.8 1.1 copy-start.13
  340.8 1.1 copy-start.16
  523.0 4.7 copy-start.3
  538.9 94.7 %copy-start.19 = (f32[1024]{0:T(1024)S(1)}, f32[1024]{0:T(1024)}, u32[]{:S(2)}) copy-start(f32[1024]{0:T(1024)} %param.33) | copy-start | bytes 12292
  538.9 94.7 %copy-start.20 = (f32[1024]{0:T(1024)S(1)}, f32[1024]{0:T(1024)}, u32[]{:S(2)}) copy-start(f32[1024]{0:T(1024)} %param.32) | copy-start | bytes 12292
  539.0 97.9 %copy-start.11 = (s32[1024]{0:T(1024)S(1)}, s32[1024]{0:T(1024)}, u32[]{:S(2)}) copy-start(s32[1024]{0:T(1024)} %copy-done.10) | copy-start | bytes 12292
  539.0 97.9 %copy-start.22 = (s32[16]{0:T(128)S(1)}, s32[16]{0:T(128)}, u32[]{:S(2)}) copy-start(s32[16]{0:T(128)} %copy-done.21) | copy-start | bytes 196
Sparse Core Ops, SparseCore 0:
  539.1 94.4 all-reduce.1
where the time goes:
time: 649 us; the launch traced here: 647 us
  waiting for transfers between devices  358 us (55%)
  matrix products  87.6 us (13%)
  local copies, waits for them, and re-layouts  66.9 us (10%)
  other arithmetic  56 us (9%)
  blocking collectives  31 us (5%)
  starting transfers between devices  29.7 us (5%)
  between operations  17.2 us (3%)
    all_to_all x1, waiting for transfers between devices, body(): lax.all_to_all(sums, 'blk', split_axis=0, concat_axis=0, tiled=True)  172 us
    psum x1, waiting for transfers between devices, body(): whole_sum = lax.psum(partial_update, 'head')  94.6 us
    all_to_all x1, waiting for transfers between devices, body(): lax.all_to_all(send_q, 'blk', split_axis=0, concat_axis=0, tiled=True)  90.9 us
    dot_general x16, matrix products, one_block(): jnp.einsum('thd,rhd->htr', block_q, cache_keys, preferred_element_type=jn...  39.2 us
    dot_general x16, matrix products, one_block(): jnp.einsum('htr,rhd->thd', weights, cache_values, preferred_element_type=...  26.9 us
    reduce_sum x17, other arithmetic, softmax_part(): return (peak, jnp.sum(weights, axis=-1), weights.astype(jnp.bfloat16))  24 us
    dynamic_update_slice x48, local copies, waits for them, and re-layouts, cache_part(): maxima, totals, sums = lax.map(one_block, (flat_q, flat_var))  16.9 us
    all_to_all x1, blocking collectives, body(): lax.all_to_all(totals, 'blk', split_axis=0, concat_axis=0, tiled=True)  16 us
  transfers between devices with their start and end apart: 4, of which 3 were waited for; matrix products, arithmetic and copies ran while one was open for 4% of the time, Pallas kernels for 0%

commit v1 on v0

--- a/solution.py
+++ b/solution.py
@@ -193,7 +193,11 @@
     )
     partial_update = jnp.dot(attended, w_out, preferred_element_type=jnp.float32)
     x_float = doc_x.astype(jnp.float32)
-    whole_sum = lax.psum(partial_update, "head")
+    whole_sum = partial_update
+    for hop in (1, 2):
+        whole_sum = whole_sum + lax.ppermute(
+            whole_sum, "head", [(dev, dev ^ hop) for dev in range(4)]
+        )
     hidden = x_float + whole_sum
     square_sum = jnp.sum(hidden * hidden, axis=1)
     weighted = jnp.sum(hidden * norm_gain * readout, axis=1)

time: 649 us -> 726 us (1.12)
  waiting for transfers between devices: 358 us -> 442 us
  between operations: 17.2 us -> 3.8 us
    ppermute x0 -> x2, waiting for transfers between devices: none -> 179 us  [body(): lax.ppermute(whole_sum, 'head', [(dev, dev ^ hop) for dev in range(4)])]
    psum x1 -> x0, waiting for transfers between devices: 94.6 us -> none  [body(): whole_sum = lax.psum(partial_update, 'head')]
    unnamed x60 -> x62, local copies, waits for them, and re-layouts: 13.3 us -> 17.2 us
  transfers between devices with their start and end apart: 4 -> 5, of which waited for: 3 -> 4; matrix products, arithmetic and copies ran while one was open for 4% -> 4% of each run, Pallas kernels for 0% -> 0%
where the time goes in v1:
time: 726 us; the launch traced here: 724 us
  waiting for transfers between devices  442 us (61%)
  matrix products  85.7 us (12%)
  local copies, waits for them, and re-layouts  68.5 us (9%)
  other arithmetic  58 us (8%)
  starting transfers between devices  33.8 us (5%)
  blocking collectives  31 us (4%)
    ppermute x2, waiting for transfers between devices, body(): lax.ppermute(whole_sum, 'head', [(dev, dev ^ hop) for dev in range(4)])  179 us
    all_to_all x1, waiting for transfers between devices, body(): lax.all_to_all(sums, 'blk', split_axis=0, concat_axis=0, tiled=True)  172 us
    all_to_all x1, waiting for transfers between devices, body(): lax.all_to_all(send_q, 'blk', split_axis=0, concat_axis=0, tiled=True)  91 us
    dot_general x16, matrix products, one_block(): jnp.einsum('thd,rhd->htr', block_q, cache_keys, preferred_element_type=jn...  39.2 us
    dot_general x16, matrix products, one_block(): jnp.einsum('htr,rhd->thd', weights, cache_values, preferred_element_type=...  26.9 us
    reduce_sum x17, other arithmetic, softmax_part(): return (peak, jnp.sum(weights, axis=-1), weights.astype(jnp.bfloat16))  24 us
    unnamed x62, local copies, waits for them, and re-layouts  17.2 us
    dynamic_update_slice x48, local copies, waits for them, and re-layouts, cache_part(): maxima, totals, sums = lax.map(one_block, (flat_q, flat_var))  16.9 us
  transfers between devices with their start and end apart: 5, of which 4 were waited for; matrix products, arithmetic and copies ran while one was open for 4% of the time, Pallas kernels for 0%

profile of v1, /device:TPU:1, one launch (start us, length us, event | category | flops | bytes accessed | tf_op | source)
XLA Modules:
  0.0 724.0 jit_solution(5790719046161424733)
XLA Ops:
  4.5 13.2 %all-to-all-start.1 = ((bf16[64,1,128]{2,1,0:T(2,128)(2,1)}), bf16[64,1,128]{2,1,0:T(2,128)(2,1)S(1)}, u32[]{:S(2)}, u32[]{:S(2)}) async-start(bf16[64,1,128]{2,1,0:T(2,128)(2,1)} %copy.108), calls=%async_computation.1 | async-start | bytes 65536 | tf_op jit(solution)/shard_map/all_to_all | solution.py:165
  19.9 2.4 fusion.63
  23.5 2.7 gather_fusion
  26.3 4.6 broadcast_select_fusion
  30.9 10.7 %all-to-all-start = ((bf16[64,128,256]{2,1,0:T(8,128)(2,1)}), bf16[64,128,256]{2,1,0:T(8,128)(2,1)}, u32[]{:S(2)}, u32[]{:S(2)}) async-start(bf16[64,128,256]{2,1,0:T(8,128)(2,1)} %broadcast_select_fusion), calls=%async_computation | async-start | bytes 8388608 | tf_op jit(solution)/shard_map/all_to_all | solution.py:164
  46.4 91.0 %all-to-all-done = bf16[64,128,256]{2,1,0:T(8,128)(2,1)} async-done(((bf16[64,128,256]{2,1,0:T(8,128)(2,1)}), bf16[64,128,256]{2,1,0:T(8,128)(2,1)}, u32[]{:S(2)}, u32[]{:S(2)}) %all-to-all-start) | async-done | bytes 4194336 | tf_op jit(solution)/shard_map/all_to_all | solution.py:164
  137.4 12.9 %reshape.307 = bf16[16,512,4,64]{3,2,1,0:T(4,128)(2,1)} reshape(bf16[64,128,256]{2,1,0:T(8,128)(2,1)} %all-to-all-done) | data formatting | bytes 8388608 | tf_op jit(solution)/shard_map/reshape | solution.py:49
  150.3 12.7 %copy.110 = bf16[16,512,4,64]{1,3,2,0:T(8,128)(2,1)} copy(bf16[16,512,4,64]{3,2,1,0:T(4,128)(2,1)} %reshape.307) | data formatting | bytes 8388608
  163.0 119.6 %while.15 = (s32[]{:T(128)}, f32[16,512,4]{1,2,0:T(4,128)S(1)}, f32[16,512,4]{1,2,0:T(4,128)S(1)}, f32[16,512,256]{2,1,0:T(8,128)}, bf16[16,512,4,64]{1,3,2,0:T(...) while((s32[]{:T(128)}, f32[16,512,4]{1,2,0:T(4,128)S(1)}, ...), condition=%wide.region_7.8_spmd.clone, body=%wide.region_4.7_spmd.clone.sunk | while | flops 288617472 | bytes 17115396 | solution.py:68
  163.8 2.5 fusion.87
  171.4 2.5 fusion.87
  178.9 2.5 fusion.87
  182.8 1.7 fusion.89
  186.3 2.4 fusion.87
  193.8 2.5 fusion.87
  201.3 2.5 fusion.87
  208.7 2.5 fusion.87
  216.2 2.5 fusion.87
  220.1 1.7 fusion.89
  223.6 2.5 fusion.87
  227.6 1.7 fusion.89
  231.1 2.5 fusion.87
  235.1 1.7 fusion.89
  238.6 2.4 fusion.87
  242.6 1.7 fusion.89
  246.1 2.5 fusion.87
  253.5 2.5 fusion.87
  257.5 1.7 fusion.89
  261.0 2.5 fusion.87
  265.0 1.7 fusion.89
  268.5 2.4 fusion.87
  276.0 2.5 fusion.87
  282.7 16.0 %all_to_all.26 = f32[64,128,4]{1,2,0:T(4,128)} all-to-all(f32[64,128,4]{1,2,0:T(4,128)S(1)} %bitcast.155), channel_id=1, replica_groups=mesh['head'=4,'blk'=64] {'blk'}, dimensions={0} | all-to-all | bytes 262144 | tf_op jit(solution)/shard_map/all_to_all | solution.py:172
  298.7 15.0 %all_to_all.27 = f32[64,128,4]{1,2,0:T(4,128)S(1)} all-to-all(f32[64,128,4]{1,2,0:T(4,128)S(1)} %bitcast.154), channel_id=1, replica_groups=mesh['head'=4,'blk'=64] {'blk'}, dimensions={0} | all-to-all | bytes 262144 | tf_op jit(solution)/shard_map/all_to_all | solution.py:171
  313.7 5.7 all-to-all-start.2
  320.8 2.6 convolution_convert_fusion
  323.4 2.8 reshape.308
  326.6 1.8 fusion.64
  333.0 172.2 %all-to-all-done.2 = f32[64,128,256]{2,1,0:T(8,128)} async-done(((f32[64,128,256]{2,1,0:T(8,128)}), f32[64,128,256]{2,1,0:T(8,128)}, u32[]{:S(2)}, u32[]{:S(2)}) %all-to-all-start.2) | async-done | bytes 8388640 | tf_op jit(solution)/shard_map/all_to_all | solution.py:173
  505.1 9.0 %copy.112 = f32[64,128,256]{1,2,0:T(8,128)} copy(f32[64,128,256]{2,1,0:T(8,128)} %all-to-all-done.2) | data formatting | bytes 16777216 | tf_op jit(solution)/shard_map/all_to_all | solution.py:173
  514.1 4.6 broadcast_multiply_fusion
  518.8 8.5 %fusion.24 = bf16[8,128,4,64]{1,0,3,2:T(8,128)(2,1)S(1)} fusion(f32[64,128,4,64]{1,3,2,0:T(8,128)S(1)} %broadcast_multiply_fusion, f32[8,4,64,128]{3,2,1,0:T(8,128)S(1)} %copy-done.3, f32[8,128,4]{1,0,2:T(8,128)S(1)} %convolution_add_fusion, f32[8,128,4]{1,0,2:T(8,128)S(1)} %get-tuple-element.200, s32[64]{0:T(128)S(1)} %copy-done.16, s32[8]{0:T(128)S(1)} %copy-done.13), kind=kOutput, calls=%fused_computation.36 | convolution fusion | flops 202375680 | bytes 9994528 | tf_op jit(solution)/shard_map/dg,dthe->gthe/dot_general | solution.py:185
  529.6 91.2 %collective-permute-done = f32[1024,1024]{0,1:T(8,128)S(1)} collective-permute-done((f32[1024,1024]{0,1:T(8,128)S(1)}, f32[1024,1024]{0,1:T(8,128)S(1)}, u32[]{:S(2)}, u32[]{:S(2)}) %collective-permute-start) | collective-permute-done | bytes 4194336 | tf_op jit(solution)/shard_map/ppermute | solution.py:198
  620.8 2.9 add.102
  623.7 2.7 collective-permute-start.1
  626.4 2.6 copy.125
  629.0 88.1 %collective-permute-done.1 = f32[1024,1024]{0,1:T(8,128)} collective-permute-done((f32[1024,1024]{0,1:T(8,128)}, f32[1024,1024]{0,1:T(8,128)}, u32[]{:S(2)}, u32[]{:S(2)}) %collective-permute-start.1) | collective-permute-done | bytes 4194336 | tf_op jit(solution)/shard_map/ppermute | solution.py:198
  717.1 4.8 multiply_reduce_fusion
  (235 shorter events, 88.0 us)
Async XLA Ops:
  0.6 526.7 %copy-start = (bf16[256,1024]{1,0:T(8,128)(2,1)S(1)}, bf16[256,1024]{1,0:T(8,128)(2,1)}, u32[]{:S(2)}) copy-start(bf16[256,1024]{1,0:T(8,128)(2,1)} %param.30) | copy-start | bytes 1572868
  1.4 318.0 %copy-start.15 = (s32[64]{0:T(128)}, s32[64]{0:T(128)S(1)}, u32[]{:S(2)}) copy-start(s32[64]{0:T(128)S(1)} %and_select_fusion) | copy-start | bytes 772
  2.3 317.1 %copy-start.12 = (s32[8]{0:T(128)}, s32[8]{0:T(128)S(1)}, u32[]{:S(2)}) copy-start(s32[8]{0:T(128)S(1)} %slice_reduce_fusion) | copy-start | bytes 100
  2.4 23.8 %copy-start.17 = (pred[64]{0:T(512)(128)(4,1)}, pred[64]{0:T(512)(128)(4,1)S(1)}, u32[]{:S(2)}) copy-start(pred[64]{0:T(512)(128)(4,1)S(1)} %compare_and_fusion) | copy-start | bytes 196
  2.5 21.1 %copy-start.14 = (s32[1024]{0:T(1024)}, s32[1024]{0:T(1024)S(1)}, u32[]{:S(2)}) copy-start(s32[1024]{0:T(1024)S(1)} %pad_clamp_fusion) | copy-start | bytes 12292
  4.5 26.4 %all-to-all-start.1 = ((bf16[64,1,128]{2,1,0:T(2,128)(2,1)}), bf16[64,1,128]{2,1,0:T(2,128)(2,1)S(1)}, u32[]{:S(2)}, u32[]{:S(2)}) async-start(bf16[64,1,128]{2,1,0:T(2,128)(2,1)} %copy.108), calls=%async_computation.1 | async-start | bytes 65536 | tf_op jit(solution)/shard_map/all_to_all | solution.py:165
  18.4 4.8 copy-start.10
  18.5 0.5 copy-start.21
  30.8 10.7 %copy-start.26 = (s32[64]{0:T(128)S(1)}, s32[64]{0:T(128)}, u32[]{:S(2)}) copy-start(s32[64]{0:T(128)} %param.23) | copy-start | bytes 772
  30.8 13.9 %copy-start.6 = (bf16[512,256]{1,0:T(8,128)(2,1)S(1)}, bf16[512,256]{1,0:T(8,128)(2,1)}, u32[]{:S(2)}) copy-start(bf16[512,256]{1,0:T(8,128)(2,1)} %param.24) | copy-start | bytes 786436
  30.8 14.1 %copy-start.7 = (bf16[512,256]{1,0:T(8,128)(2,1)S(1)}, bf16[512,256]{1,0:T(8,128)(2,1)}, u32[]{:S(2)}) copy-start(bf16[512,256]{1,0:T(8,128)(2,1)} %param.25) | copy-start | bytes 786436
  30.8 14.3 %copy-start.27 = (s32[8]{0:T(128)S(1)}, s32[8]{0:T(128)}, u32[]{:S(2)}) copy-start(s32[8]{0:T(128)} %param.22) | copy-start | bytes 100
  30.8 14.8 %copy-start.23 = (f32[2,4]{1,0:T(2,128)S(1)}, f32[2,4]{1,0:T(2,128)}, u32[]{:S(2)}) copy-start(f32[2,4]{1,0:T(2,128)} %param.31) | copy-start | bytes 100
  30.9 106.5 %all-to-all-start = ((bf16[64,128,256]{2,1,0:T(8,128)(2,1)}), bf16[64,128,256]{2,1,0:T(8,128)(2,1)}, u32[]{:S(2)}, u32[]{:S(2)}) async-start(bf16[64,128,256]{2,1,0:T(8,128)(2,1)} %broadcast_select_fusion), calls=%async_computation | async-start | bytes 8388608 | tf_op jit(solution)/shard_map/all_to_all | solution.py:164
  150.3 12.7 %copy-start.8 = (s32[512]{0:T(512)S(1)}, s32[512]{0:T(512)}, u32[]{:S(2)}) copy-start(s32[512]{0:T(512)} %param.26) | copy-start | bytes 6148
  313.7 7.2 copy-start.1
  313.7 191.5 %all-to-all-start.2 = ((f32[64,128,256]{2,1,0:T(8,128)}), f32[64,128,256]{2,1,0:T(8,128)}, u32[]{:S(2)}, u32[]{:S(2)}) async-start(f32[64,128,256]{2,1,0:T(8,128)} %bitcast.145), calls=%async_computation.2 | async-start | bytes 16777216 | tf_op jit(solution)/shard_map/all_to_all | solution.py:173
  319.4 6.8 copy-start.9
  319.4 6.8 copy-start.2
  326.1 2.4 copy-start.24
  326.2 2.4 copy-start.25
  328.6 1.3 copy-start.4
  331.6 1.0 copy-start.5
  331.6 1.0 copy-start.18
  331.6 1.1 copy-start.13
  331.6 1.1 copy-start.16
  514.1 4.7 copy-start.3
  528.1 92.8 %collective-permute-start = (f32[1024,1024]{0,1:T(8,128)S(1)}, f32[1024,1024]{0,1:T(8,128)S(1)}, u32[]{:S(2)}, u32[]{:S(2)}) collective-permute-start(f32[1024,1024]{0,1:T(8,128)S(1)} %fusion.34), channel_id=1, source_target_pairs={{0,64},{64,0},{128,192},{192,128},{1,65},{65,1},{129,193},{193,129... | collective-permute-start | bytes 12582920 | tf_op jit(solution)/shard_map/ppermute | solution.py:198
  623.7 93.4 %copy-start.19 = (f32[1024]{0:T(1024)S(1)}, f32[1024]{0:T(1024)}, u32[]{:S(2)}) copy-start(f32[1024]{0:T(1024)} %param.33) | copy-start | bytes 12292
  623.7 93.4 %copy-start.20 = (f32[1024]{0:T(1024)S(1)}, f32[1024]{0:T(1024)}, u32[]{:S(2)}) copy-start(f32[1024]{0:T(1024)} %param.32) | copy-start | bytes 12292
  623.7 93.4 %collective-permute-start.1 = (f32[1024,1024]{0,1:T(8,128)}, f32[1024,1024]{0,1:T(8,128)}, u32[]{:S(2)}, u32[]{:S(2)}) collective-permute-start(f32[1024,1024]{0,1:T(8,128)} %add.102), channel_id=1, source_target_pairs={{0,128},{64,192},{128,0},{192,64},{1,129},{65,193},{129,1},{193,65... | collective-permute-start | bytes 12582920 | tf_op jit(solution)/shard_map/ppermute | solution.py:198
  721.8 1.4 copy-start.11
  721.9 1.4 copy-start.22
